TPU v7x, 256 devices: a whole 4x4x8 slice. The times are simulated.
256 devices in a mesh: head: 16 (over y, x_lo, core), ctx: 16 (over x_hi, z).
Axes of the slice: x: 4 (x_hi: 2, x_lo: 2; x = x_hi * 2 + x_lo), y: 4, z: 8, core: 2. Of those that a mesh axis runs over, the one named last changes fastest.
Arguments:
- queries: bfloat16 [65536, 2048], P(('ctx', 'head')), may hold values from -6 to 6
- keys: bfloat16 [65536, 2048], P(('ctx', 'head')), may hold values from -6 to 6
- values: bfloat16 [65536, 2048], P(('ctx', 'head')), may hold values from -24 to 24
- picks: int32 [128, 2], replicated, may hold values from 0 to 127, as said below
Outputs:
- attended: bfloat16 [65536, 2048], P(('ctx', 'head'))
Inputs may be any that keep to these rules, and one draw needn't show every extreme that they name: `picks`: rows 8 * c to 8 * c + 7 are the query blocks held by index c of ctx, and blocks 8 * o to 8 * o + 7 are held by index o. Among the 16 entries of one such group of rows, at most 2 name blocks held by any one index of ctx; one index o, the same for every group, is named exactly 2 times by every group.
All inputs are finite; a program needn't handle non-finite values.
Results may differ from a plain program's by a relative error of at most 0.0039.
Values may be sent and summed in bfloat16 or wider, within the bound.
A program may use at most 128 MiB of HBM per device.

v0:
```python
import math
import jax
import jax.numpy as jnp
from jax import lax
from jax.sharding import PartitionSpec as P

HEADS = 16
HD = 128
BLOCK = 512
RSEL = 2


def block_pair(query_block, key_block, value_block, score_scale):
    scores = (
        jnp.einsum("qhd,khd->hqk", query_block, key_block, preferred_element_type=jnp.float32)
        * score_scale
    )
    row_max = jnp.max(scores, axis=-1)
    exponent = jnp.exp(scores - row_max[..., None])
    row_sum = jnp.sum(exponent, axis=-1)
    weights = exponent.astype(jnp.bfloat16)
    partial_out = jnp.einsum(
        "hqk,khd->qhd", weights, value_block, preferred_element_type=jnp.float32
    )
    return (partial_out, row_max, row_sum)


def route_tables(picks, local_blocks, ctx_count):
    slots = local_blocks * RSEL
    owners = (picks // local_blocks).reshape(ctx_count, slots)
    within = (picks % local_blocks).reshape(ctx_count, slots)
    owner_ids = jnp.arange(ctx_count, dtype=jnp.int32)
    one_hot = (owners[:, :, None] == owner_ids[None, None, :]).astype(jnp.int32)
    running = jnp.cumsum(one_hot, axis=1)
    position = jnp.sum(one_hot * running, axis=-1) - 1
    return (owners, within, position)


def local(queries, keys, values, picks):
    head_count = lax.axis_size("head")
    ctx_count = lax.axis_size("ctx")
    my_index = lax.axis_index("ctx")
    heads_here = HEADS // head_count
    tok_rows = queries.shape[0]
    score_scale = 1.0 / math.sqrt(HD)
    q_split = queries.reshape(tok_rows, HEADS, HD)
    k_split = keys.reshape(tok_rows, HEADS, HD)
    v_split = values.reshape(tok_rows, HEADS, HD)
    q_heads, k_heads, v_heads = (
        lax.all_to_all(q_split, "head", split_axis=1, concat_axis=0, tiled=True),
        lax.all_to_all(k_split, "head", split_axis=1, concat_axis=0, tiled=True),
        lax.all_to_all(v_split, "head", split_axis=1, concat_axis=0, tiled=True),
    )
    local_blocks = q_heads.shape[0] // BLOCK
    q_blocks = q_heads.reshape(local_blocks, BLOCK, heads_here, HD)
    k_blocks = k_heads.reshape(local_blocks, BLOCK, heads_here, HD)
    v_blocks = v_heads.reshape(local_blocks, BLOCK, heads_here, HD)
    capacity = (local_blocks * RSEL + ctx_count - 1) // ctx_count + 1
    slots = local_blocks * RSEL
    owners, within, position = route_tables(picks, local_blocks, ctx_count)
    mine_owner = lax.dynamic_index_in_dim(owners, my_index, 0, keepdims=False)
    mine_pos = lax.dynamic_index_in_dim(position, my_index, 0, keepdims=False)
    slot_ids = jnp.arange(capacity, dtype=jnp.int32)
    asked = (owners == my_index)[:, :, None] & (position[:, :, None] == slot_ids[None, None, :])
    wanted = jnp.sum(asked.astype(jnp.int32) * within[:, :, None], axis=1)
    pick_back = mine_owner * capacity + mine_pos

    def own_pair(blocks):
        return block_pair(blocks[0], blocks[1], blocks[2], score_scale)

    own_out, own_max, own_sum = lax.map(own_pair, (q_blocks, k_blocks, v_blocks))
    owner_ids = jnp.arange(ctx_count, dtype=jnp.int32)
    chosen = (mine_owner[:, None, None] == owner_ids[None, :, None]) & (
        mine_pos[:, None, None] == slot_ids[None, None, :]
    )
    query_of_slot = jnp.arange(slots, dtype=jnp.int32) // RSEL
    source_block = jnp.sum(chosen.astype(jnp.int32) * query_of_slot[:, None, None], axis=0)
    send_queries = q_blocks[source_block]
    arrived = lax.all_to_all(send_queries, "ctx", split_axis=0, concat_axis=0, tiled=True)
    arrived_flat = arrived.reshape(ctx_count * capacity, BLOCK, heads_here, HD)

    def owner_pair(items):
        query_block, block_index = items
        return block_pair(query_block, k_blocks[block_index], v_blocks[block_index], score_scale)

    remote_out, remote_max, remote_sum = lax.map(owner_pair, (arrived_flat, wanted.reshape(-1)))
    remote_out = remote_out.reshape(ctx_count, capacity, BLOCK, heads_here, HD)
    remote_max = remote_max.reshape(ctx_count, capacity, heads_here, BLOCK)
    remote_sum = remote_sum.reshape(ctx_count, capacity, heads_here, BLOCK)
    back_out, back_max, back_sum = (
        lax.all_to_all(remote_out, "ctx", split_axis=0, concat_axis=0, tiled=True),
        lax.all_to_all(remote_max, "ctx", split_axis=0, concat_axis=0, tiled=True),
        lax.all_to_all(remote_sum, "ctx", split_axis=0, concat_axis=0, tiled=True),
    )
    far_out = back_out.reshape(ctx_count * capacity, BLOCK, heads_here, HD)[pick_back]
    far_max = back_max.reshape(ctx_count * capacity, heads_here, BLOCK)[pick_back]
    far_sum = back_sum.reshape(ctx_count * capacity, heads_here, BLOCK)[pick_back]
    far_out = far_out.reshape(local_blocks, RSEL, BLOCK, heads_here, HD)
    far_max = far_max.reshape(local_blocks, RSEL, heads_here, BLOCK)
    far_sum = far_sum.reshape(local_blocks, RSEL, heads_here, BLOCK)
    overall = jnp.maximum(own_max, jnp.max(far_max, axis=1))
    own_factor = jnp.exp(own_max - overall)
    far_factor = jnp.exp(far_max - overall[:, None])
    numer = own_out * jnp.transpose(own_factor, (0, 2, 1))[..., None]
    numer = numer + jnp.sum(far_out * jnp.transpose(far_factor, (0, 1, 3, 2))[..., None], axis=1)
    denom = own_sum * own_factor + jnp.sum(far_sum * far_factor, axis=1)
    result = (numer / jnp.transpose(denom, (0, 2, 1))[..., None]).astype(jnp.bfloat16)
    result = result.reshape(local_blocks * BLOCK, heads_here, HD)
    restored = lax.all_to_all(result, "head", split_axis=0, concat_axis=1, tiled=True)
    return restored.reshape(tok_rows, HEADS * HD)


def solution(mesh):
    placed = (P(("ctx", "head"), None), P(("ctx", "head"), None), P(("ctx", "head"), None), P())
    return jax.shard_map(
        local, mesh=mesh, in_specs=placed, out_specs=P(("ctx", "head"), None), check_vma=False
    )
```

profile of v0, /device:TPU:164, one launch (start us, length us, event | category | flops | bytes accessed | tf_op | source)
XLA Modules:
  0.0 586.6 jit_solution(18382969166931936499)
XLA Ops:
  0.0 2.4 copy.120
  2.4 5.2 all-to-all-start.1
  8.9 15.3 %all-to-all-done.1 = bf16[256,16,128]{0,2,1:T(8,128)(2,1)S(1)} async-done(((bf16[256,16,128]{0,2,1:T(8,128)(2,1)}), bf16[256,16,128]{0,2,1:T(8,128)(2,1)S(1)}, u32[]{:S(2)}, u32[]{:S(2)}) %all-to-all-start.1) | async-done | bytes 1048608 | tf_op jit(solution)/shard_map/all_to_all | solution.py:50
  24.2 3.7 all-to-all-start
  28.2 2.3 copy.122
  31.1 13.3 %all-to-all-done = bf16[256,16,128]{0,2,1:T(8,128)(2,1)S(1)} async-done(((bf16[256,16,128]{0,2,1:T(8,128)(2,1)}), bf16[256,16,128]{0,2,1:T(8,128)(2,1)S(1)}, u32[]{:S(2)}, u32[]{:S(2)}) %all-to-all-start) | async-done | bytes 1048608 | tf_op jit(solution)/shard_map/all_to_all | solution.py:52
  44.4 4.3 all-to-all-start.2
  49.8 3.1 gather_fusion
  52.9 12.5 %all-to-all-done.2 = bf16[256,16,128]{0,2,1:T(8,128)(2,1)} async-done(((bf16[256,16,128]{0,2,1:T(8,128)(2,1)}), bf16[256,16,128]{0,2,1:T(8,128)(2,1)}, u32[]{:S(2)}, u32[]{:S(2)}) %all-to-all-start.2) | async-done | bytes 1048608 | tf_op jit(solution)/shard_map/all_to_all | solution.py:51
  65.4 9.2 %all-to-all-start.3 = ((bf16[16,2,512,1,128]{4,2,1,3,0:T(8,128)(2,1)}), bf16[16,2,512,1,128]{4,2,1,3,0:T(8,128)(2,1)}, u32[]{:S(2)}, u32[]{:S(2)}) async-start(bf16[16,2,512,1,128]{4,2,1,3,0:T(8,128)(2,1)} %bitcast.142), calls=%async_computation.3 | async-start | bytes 8388608 | tf_op jit(solution)/shard_map/all_to_all | solution.py:79
  75.8 1.6 copy.123
  77.4 89.8 %all-to-all-done.3 = bf16[16,2,512,1,128]{4,2,1,3,0:T(8,128)(2,1)} async-done(((bf16[16,2,512,1,128]{4,2,1,3,0:T(8,128)(2,1)}), bf16[16,2,512,1,128]{4,2,1,3,0:T(8,128)(2,1)}, u32[]{:S(2)}, u32[]{:S(2)}) %all-to-all-start.3) | async-done | bytes 4194336 | tf_op jit(solution)/shard_map/all_to_all | solution.py:79
  167.2 152.0 %while.29 = (s32[]{:T(128)}, f32[32,512,1,128]{1,3,2,0:T(8,128)}, f32[32,1,512]{2,1,0:T(1,128)S(1)}, f32[32,1,512]{2,1,0:T(1,128)S(1)}, s32[32]{0:T(128)S(1)}, /...) while((s32[]{:T(128)}, f32[32,512,1,128]{1,3,2,0:T(8,128)}, ...), condition=%wide.region_11.12_spmd, body=%wide.region_8.11_spmd.sunk | while | flops 135789568 | bytes 3818663 | solution.py:86
  320.0 10.7 %all-to-all-start.4 = ((f32[16,2,1,512]{3,1,2,0:T(2,128)}), f32[16,2,1,512]{3,1,2,0:T(2,128)S(1)}, u32[]{:S(2)}, u32[]{:S(2)}) async-start(f32[16,2,1,512]{3,1,2,0:T(2,128)} %reshape.320), calls=%async_computation.4 | async-start | bytes 131072 | tf_op jit(solution)/shard_map/all_to_all | solution.py:92
  330.9 3.6 all-to-all-done.4
  334.5 12.6 %all_to_all.80 = f32[16,2,1,512]{3,1,2,0:T(2,128)S(1)} all-to-all(f32[16,2,1,512]{3,1,2,0:T(2,128)S(1)} %reshape.326), channel_id=1, replica_groups=mesh['head'=16,'ctx'=16] {'ctx'}, dimensions={0} | all-to-all | bytes 131072 | tf_op jit(solution)/shard_map/all_to_all | solution.py:93
  347.1 10.9 %all-to-all-start.5 = ((f32[16,2,512,1,128]{2,4,1,3,0:T(8,128)}), f32[16,2,512,1,128]{2,4,1,3,0:T(8,128)}, u32[]{:S(2)}, u32[]{:S(2)}) async-start(f32[16,2,512,1,128]{2,4,1,3,0:T(8,128)} %bitcast.144), calls=%async_computation.5 | async-start | bytes 16777216 | tf_op jit(solution)/shard_map/all_to_all | solution.py:91
  358.0 12.5 %while.28 = (s32[]{:T(128)}, f32[8,512,1,128]{1,3,2,0:T(8,128)}, f32[8,1,512]{2,1,0:T(1,128)S(1)}, f32[8,1,512]{2,1,0:T(1,128)S(1)}, bf16[8,512,1,128]{3,1,2,0:T...) while((s32[]{:T(128)}, f32[8,512,1,128]{1,3,2,0:T(8,128)}, ...), condition=%wide.region_3.4_spmd, body=%wide.region_0.3_spmd.sunk | while | flops 135789568 | bytes 3819609 | solution.py:71
  372.1 176.6 %all-to-all-done.5 = f32[16,2,512,1,128]{2,4,1,3,0:T(8,128)} async-done(((f32[16,2,512,1,128]{2,4,1,3,0:T(8,128)}), f32[16,2,512,1,128]{2,4,1,3,0:T(8,128)}, u32[]{:S(2)}, u32[]{:S(2)}) %all-to-all-start.5) | async-done | bytes 8388640 | tf_op jit(solution)/shard_map/all_to_all | solution.py:91
  548.7 6.2 %gather_fusion.2 = f32[16,512,128]{1,2,0:T(8,128)} fusion(f32[32,512,128]{1,2,0:T(8,128)} %bitcast.44, s32[1024]{0:T(1024)S(1)} %pad_clamp_fusion), kind=kCustom, calls=%fused_computation.2 | custom fusion | bytes 8388672 | tf_op jit(solution)/shard_map/gather | solution.py:95
  554.9 3.1 multiply_reduce_fusion
  559.8 1.4 reduce.19
  561.5 21.9 %all_to_all.81 = bf16[16,2,16384]{2,1,0:T(2,128)(2,1)S(1)} all-to-all(bf16[16,2,16384]{2,1,0:T(2,128)(2,1)S(1)} %reshape.387), channel_id=1, replica_groups=mesh['head'=16,'ctx'=16] {'head'}, dimensions={0} | all-to-all | bytes 2097152 | tf_op jit(solution)/shard_map/all_to_all | solution.py:109
  585.1 1.4 copy.143
  (256 shorter events, 120.7 us)
Async XLA Ops:
  0.0 7.6 %copy-start.1 = (bf16[256,2048]{1,0:T(8,128)(2,1)S(1)}, bf16[256,2048]{1,0:T(8,128)(2,1)}, u32[]{:S(2)}) copy-start(bf16[256,2048]{1,0:T(8,128)(2,1)} %param.10) | copy-start | bytes 3145732
  0.0 27.9 %copy-start.2 = (s32[128,2]{0,1:T(2,128)S(1)}, s32[128,2]{0,1:T(2,128)}, u32[]{:S(2)}) copy-start(s32[128,2]{0,1:T(2,128)} %param.11) | copy-start | bytes 3076
  2.4 21.8 %all-to-all-start.1 = ((bf16[256,16,128]{0,2,1:T(8,128)(2,1)}), bf16[256,16,128]{0,2,1:T(8,128)(2,1)S(1)}, u32[]{:S(2)}, u32[]{:S(2)}) async-start(bf16[256,16,128]{0,2,1:T(8,128)(2,1)} %bitcast.22), calls=%async_computation.1 | async-start | bytes 2097152 | tf_op jit(solution)/shard_map/all_to_all | solution.py:50
  24.2 20.2 %all-to-all-start = ((bf16[256,16,128]{0,2,1:T(8,128)(2,1)}), bf16[256,16,128]{0,2,1:T(8,128)(2,1)S(1)}, u32[]{:S(2)}, u32[]{:S(2)}) async-start(bf16[256,16,128]{0,2,1:T(8,128)(2,1)} %bitcast.17), calls=%async_computation | async-start | bytes 2097152 | tf_op jit(solution)/shard_map/all_to_all | solution.py:52
  44.4 21.0 %all-to-all-start.2 = ((bf16[256,16,128]{0,2,1:T(8,128)(2,1)}), bf16[256,16,128]{0,2,1:T(8,128)(2,1)}, u32[]{:S(2)}, u32[]{:S(2)}) async-start(bf16[256,16,128]{0,2,1:T(8,128)(2,1)} %bitcast.27), calls=%async_computation.2 | async-start | bytes 2097152 | tf_op jit(solution)/shard_map/all_to_all | solution.py:51
  65.4 101.9 %all-to-all-start.3 = ((bf16[16,2,512,1,128]{4,2,1,3,0:T(8,128)(2,1)}), bf16[16,2,512,1,128]{4,2,1,3,0:T(8,128)(2,1)}, u32[]{:S(2)}, u32[]{:S(2)}) async-start(bf16[16,2,512,1,128]{4,2,1,3,0:T(8,128)(2,1)} %bitcast.142), calls=%async_computation.3 | async-start | bytes 8388608 | tf_op jit(solution)/shard_map/all_to_all | solution.py:79
  320.0 14.5 %all-to-all-start.4 = ((f32[16,2,1,512]{3,1,2,0:T(2,128)}), f32[16,2,1,512]{3,1,2,0:T(2,128)S(1)}, u32[]{:S(2)}, u32[]{:S(2)}) async-start(f32[16,2,1,512]{3,1,2,0:T(2,128)} %reshape.320), calls=%async_computation.4 | async-start | bytes 131072 | tf_op jit(solution)/shard_map/all_to_all | solution.py:92
  347.1 201.6 %all-to-all-start.5 = ((f32[16,2,512,1,128]{2,4,1,3,0:T(8,128)}), f32[16,2,512,1,128]{2,4,1,3,0:T(8,128)}, u32[]{:S(2)}, u32[]{:S(2)}) async-start(f32[16,2,512,1,128]{2,4,1,3,0:T(8,128)} %bitcast.144), calls=%async_computation.5 | async-start | bytes 16777216 | tf_op jit(solution)/shard_map/all_to_all | solution.py:91
  554.9 3.2 copy-start
where the time goes:
time: 589 us; the launch traced here: 587 us
  waiting for transfers between devices  311 us (53%)
  matrix products  83 us (14%)
  loops' own time  54.6 us (9%)
  local copies, waits for them, and re-layouts  44.7 us (8%)
  starting transfers between devices  43.9 us (7%)
  blocking collectives  34.4 us (6%)
  other arithmetic  14.5 us (2%)
    all_to_all x1, waiting for transfers between devices, local(): lax.all_to_all(remote_out, 'ctx', split_axis=0, concat_axis=0, tiled=True)  177 us
    all_to_all x1, waiting for transfers between devices, local(): lax.all_to_all(send_queries, 'ctx', split_axis=0, concat_axis=0, tiled=True)  89.8 us
    another operation x1, loops' own time, local(): lax.map(owner_pair, (arrived_flat, wanted.reshape(-1)))  54.5 us
    dot_general x40, matrix products, block_pair(): jnp.einsum('qhd,khd->hqk', query_block, key_block, preferred_element_type...  41.5 us
    dot_general x40, matrix products, block_pair(): jnp.einsum('hqk,khd->qhd', weights, value_block, preferred_element_type=j...  41.5 us
    all_to_all x1, blocking collectives, local(): lax.all_to_all(result, 'head', split_axis=0, concat_axis=1, tiled=True)  21.9 us
    dynamic_slice x32, local copies, waits for them, and re-layouts, local(): lax.map(owner_pair, (arrived_flat, wanted.reshape(-1)))  18.6 us
    all_to_all x1, waiting for transfers between devices, local(): lax.all_to_all(q_split, 'head', split_axis=1, concat_axis=0, tiled=True)  15.3 us
  transfers between devices with their start and end apart: 6, of which 6 were waited for; matrix products, arithmetic and copies ran while one was open for 4% of the time, Pallas kernels for 0%

commit v1 on v0

--- a/solution.py
+++ b/solution.py
@@ -1,3 +1,4 @@
+import functools
 import math
 import jax
 import jax.numpy as jnp
@@ -8,6 +9,16 @@
 HD = 128
 BLOCK = 512
 RSEL = 2
+
+
+def _advance_lots_all(inp, ndim_at, axis_k):
+    return jnp.concatenate(
+        lax.all_to_all(jnp.stack(jnp.split(inp, lax.axis_size("head"), ndim_at), 0), "head", 0, 0),
+        axis_k,
+    )
+
+
+time_sheet_all = functools.partial(_advance_lots_all, ndim_at=1, axis_k=0)
 
 
 def block_pair(query_block, key_block, value_block, score_scale):
@@ -49,7 +60,7 @@
     q_heads, k_heads, v_heads = (
         lax.all_to_all(q_split, "head", split_axis=1, concat_axis=0, tiled=True),
         lax.all_to_all(k_split, "head", split_axis=1, concat_axis=0, tiled=True),
-        lax.all_to_all(v_split, "head", split_axis=1, concat_axis=0, tiled=True),
+        time_sheet_all(v_split),
     )
     local_blocks = q_heads.shape[0] // BLOCK
     q_blocks = q_heads.reshape(local_blocks, BLOCK, heads_here, HD)

time: 589 us -> 606 us (1.029)
  local copies, waits for them, and re-layouts: 44.7 us -> 53.3 us
  loops' own time: 54.6 us -> 62.7 us
    another operation x1, loops' own time: 54.5 us -> 62.7 us  [local(): lax.map(owner_pair, (arrived_flat, wanted.reshape(-1)))]
    unnamed x14 -> x33, local copies, waits for them, and re-layouts: 7.43 us -> 15.2 us
where the time goes in v1:
time: 606 us; the launch traced here: 603 us
  waiting for transfers between devices  312 us (51%)
  matrix products  83 us (14%)
  loops' own time  62.7 us (10%)
  local copies, waits for them, and re-layouts  53.3 us (9%)
  starting transfers between devices  43.2 us (7%)
  blocking collectives  34.4 us (6%)
  other arithmetic  14.5 us (2%)
    all_to_all x1, waiting for transfers between devices, local(): lax.all_to_all(remote_out, 'ctx', split_axis=0, concat_axis=0, tiled=True)  177 us
    all_to_all x1, waiting for transfers between devices, local(): lax.all_to_all(send_queries, 'ctx', split_axis=0, concat_axis=0, tiled=True)  89.8 us
    another operation x1, loops' own time, local(): lax.map(owner_pair, (arrived_flat, wanted.reshape(-1)))  62.7 us
    dot_general x40, matrix products, block_pair(): jnp.einsum('qhd,khd->hqk', query_block, key_block, preferred_element_type...  41.5 us
    dot_general x40, matrix products, block_pair(): jnp.einsum('hqk,khd->qhd', weights, value_block, preferred_element_type=j...  41.5 us
    all_to_all x1, blocking collectives, local(): lax.all_to_all(result, 'head', split_axis=0, concat_axis=1, tiled=True)  21.9 us
    dynamic_slice x32, local copies, waits for them, and re-layouts, local(): lax.map(owner_pair, (arrived_flat, wanted.reshape(-1)))  18.8 us
    all_to_all x1, waiting for transfers between devices, _advance_lots_all(): lax.all_to_all(jnp.stack(jnp.split(inp, lax.axis_size('head'), ndim_at),...  15.3 us
  transfers between devices with their start and end apart: 6, of which 6 were waited for; matrix products, arithmetic and copies ran while one was open for 4% of the time, Pallas kernels for 0%

profile of v1, /device:TPU:164, one launch (start us, length us, event | category | flops | bytes accessed | tf_op | source)
XLA Modules:
  0.0 603.5 jit_solution(2851045664009216031)
XLA Ops:
  0.0 1.6 copy.148
  11.7 5.2 all-to-all-start
  18.3 15.3 %all-to-all-done = bf16[16,256,1,128]{1,3,2,0:T(8,128)(2,1)S(1)} async-done(((bf16[16,256,1,128]{1,3,2,0:T(8,128)(2,1)}), bf16[16,256,1,128]{1,3,2,0:T(8,128)(2,1)S(1)}, u32[]{:S(2)}, u32[]{:S(2)}) %all-to-all-start) | async-done | bytes 1048608 | tf_op jit(solution)/shard_map/all_to_all | solution.py:16
  33.6 3.7 all-to-all-start.1
  37.5 1.3 copy.152
  39.5 14.2 %all-to-all-done.1 = bf16[256,16,128]{0,2,1:T(8,128)(2,1)S(1)} async-done(((bf16[256,16,128]{0,2,1:T(8,128)(2,1)}), bf16[256,16,128]{0,2,1:T(8,128)(2,1)S(1)}, u32[]{:S(2)}, u32[]{:S(2)}) %all-to-all-start.1) | async-done | bytes 1048608 | tf_op jit(solution)/shard_map/all_to_all | solution.py:61
  53.8 3.7 all-to-all-start.2
  58.5 3.1 gather_fusion
  61.6 12.4 %all-to-all-done.2 = bf16[256,16,128]{0,2,1:T(8,128)(2,1)S(1)} async-done(((bf16[256,16,128]{0,2,1:T(8,128)(2,1)}), bf16[256,16,128]{0,2,1:T(8,128)(2,1)S(1)}, u32[]{:S(2)}, u32[]{:S(2)}) %all-to-all-start.2) | async-done | bytes 1048608 | tf_op jit(solution)/shard_map/all_to_all | solution.py:62
  74.0 9.2 %all-to-all-start.3 = ((bf16[16,2,512,1,128]{4,2,1,3,0:T(8,128)(2,1)}), bf16[16,2,512,1,128]{4,2,1,3,0:T(8,128)(2,1)}, u32[]{:S(2)}, u32[]{:S(2)}) async-start(bf16[16,2,512,1,128]{4,2,1,3,0:T(8,128)(2,1)} %bitcast.203), calls=%async_computation.3 | async-start | bytes 8388608 | tf_op jit(solution)/shard_map/all_to_all | solution.py:90
  84.4 1.6 copy.149
  86.1 89.8 %all-to-all-done.3 = bf16[16,2,512,1,128]{4,2,1,3,0:T(8,128)(2,1)} async-done(((bf16[16,2,512,1,128]{4,2,1,3,0:T(8,128)(2,1)}), bf16[16,2,512,1,128]{4,2,1,3,0:T(8,128)(2,1)}, u32[]{:S(2)}, u32[]{:S(2)}) %all-to-all-start.3) | async-done | bytes 4194336 | tf_op jit(solution)/shard_map/all_to_all | solution.py:90
  175.9 160.3 %while.29 = (s32[]{:T(128)}, f32[32,512,1,128]{1,3,2,0:T(8,128)}, f32[32,1,512]{2,1,0:T(1,128)S(1)}, f32[32,1,512]{2,1,0:T(1,128)S(1)}, s32[32]{0:T(128)S(1)}, /...) while((s32[]{:T(128)}, f32[32,512,1,128]{1,3,2,0:T(8,128)}, ...), condition=%wide.region_11.12_spmd, body=%wide.region_8.11_spmd.sunk | while | flops 135789568 | bytes 3818663 | solution.py:97
  337.0 10.6 %all-to-all-start.4 = ((f32[16,2,1,512]{3,1,2,0:T(2,128)}), f32[16,2,1,512]{3,1,2,0:T(2,128)S(1)}, u32[]{:S(2)}, u32[]{:S(2)}) async-start(f32[16,2,1,512]{3,1,2,0:T(2,128)} %reshape.315), calls=%async_computation.4 | async-start | bytes 131072 | tf_op jit(solution)/shard_map/all_to_all | solution.py:103
  347.8 3.6 all-to-all-done.4
  351.4 12.6 %all_to_all.70 = f32[16,2,1,512]{3,1,2,0:T(2,128)S(1)} all-to-all(f32[16,2,1,512]{3,1,2,0:T(2,128)S(1)} %reshape.321), channel_id=1, replica_groups=mesh['head'=16,'ctx'=16] {'ctx'}, dimensions={0} | all-to-all | bytes 131072 | tf_op jit(solution)/shard_map/all_to_all | solution.py:104
  364.0 10.9 %all-to-all-start.5 = ((f32[16,2,512,1,128]{2,4,1,3,0:T(8,128)}), f32[16,2,512,1,128]{2,4,1,3,0:T(8,128)}, u32[]{:S(2)}, u32[]{:S(2)}) async-start(f32[16,2,512,1,128]{2,4,1,3,0:T(8,128)} %bitcast.205), calls=%async_computation.5 | async-start | bytes 16777216 | tf_op jit(solution)/shard_map/all_to_all | solution.py:102
  374.9 12.5 %while.28 = (s32[]{:T(128)}, f32[8,512,1,128]{1,3,2,0:T(8,128)}, f32[8,1,512]{2,1,0:T(1,128)S(1)}, f32[8,1,512]{2,1,0:T(1,128)S(1)}, bf16[8,512,1,128]{3,1,2,0:T...) while((s32[]{:T(128)}, f32[8,512,1,128]{1,3,2,0:T(8,128)}, ...), condition=%wide.region_3.4_spmd, body=%wide.region_0.3_spmd.sunk | while | flops 135789568 | bytes 3819609 | solution.py:82
  389.0 176.6 %all-to-all-done.5 = f32[16,2,512,1,128]{2,4,1,3,0:T(8,128)} async-done(((f32[16,2,512,1,128]{2,4,1,3,0:T(8,128)}), f32[16,2,512,1,128]{2,4,1,3,0:T(8,128)}, u32[]{:S(2)}, u32[]{:S(2)}) %all-to-all-start.5) | async-done | bytes 8388640 | tf_op jit(solution)/shard_map/all_to_all | solution.py:102
  565.6 6.2 %gather_fusion.2 = f32[16,512,128]{1,2,0:T(8,128)} fusion(f32[32,512,128]{1,2,0:T(8,128)} %bitcast.58, s32[1024]{0:T(1024)S(1)} %pad_clamp_fusion), kind=kCustom, calls=%fused_computation.2 | custom fusion | bytes 8388672 | tf_op jit(solution)/shard_map/gather | solution.py:106
  571.8 3.1 multiply_reduce_fusion
  576.7 1.4 reduce.19
  578.5 21.9 %all_to_all.71 = bf16[16,2,16384]{2,1,0:T(2,128)(2,1)S(1)} all-to-all(bf16[16,2,16384]{2,1,0:T(2,128)(2,1)S(1)} %reshape.382), channel_id=1, replica_groups=mesh['head'=16,'ctx'=16] {'head'}, dimensions={0} | all-to-all | bytes 2097152 | tf_op jit(solution)/shard_map/all_to_all | solution.py:120
  602.1 1.4 copy.173
  (276 shorter events, 131.0 us)
Async XLA Ops:
  0.0 17.0 %copy-start.2 = (bf16[256,2048]{1,0:T(8,128)(2,1)S(1)}, bf16[256,2048]{1,0:T(8,128)(2,1)}, u32[]{:S(2)}) copy-start(bf16[256,2048]{1,0:T(8,128)(2,1)} %param.8) | copy-start | bytes 3145732
  1.6 35.6 %copy-start.4 = (s32[128,2]{0,1:T(2,128)S(1)}, s32[128,2]{0,1:T(2,128)}, u32[]{:S(2)}) copy-start(s32[128,2]{0,1:T(2,128)} %param.11) | copy-start | bytes 3076
  2.2 35.3 %copy-start.3 = (bf16[256,2048]{1,0:T(8,128)(2,1)S(1)}, bf16[256,2048]{1,0:T(8,128)(2,1)}, u32[]{:S(2)}) copy-start(bf16[256,2048]{1,0:T(8,128)(2,1)} %param.9) | copy-start | bytes 3145732
  11.7 21.8 %all-to-all-start = ((bf16[16,256,1,128]{1,3,2,0:T(8,128)(2,1)}), bf16[16,256,1,128]{1,3,2,0:T(8,128)(2,1)S(1)}, u32[]{:S(2)}, u32[]{:S(2)}) async-start(bf16[16,256,1,128]{1,3,2,0:T(8,128)(2,1)} %fusion.29), calls=%async_computation | async-start | bytes 2097152 | tf_op jit(solution)/shard_map/all_to_all | solution.py:16
  33.6 24.3 %copy-start = (bf16[16,256,1,128]{1,3,2,0:T(8,128)(2,1)}, bf16[16,256,1,128]{1,3,2,0:T(8,128)(2,1)S(1)}, u32[]{:S(2)}) copy-start(bf16[16,256,1,128]{1,3,2,0:T(8,128)(2,1)S(1)} %all-to-all-done) | copy-start | bytes 3145732
  33.6 20.2 %all-to-all-start.1 = ((bf16[256,16,128]{0,2,1:T(8,128)(2,1)}), bf16[256,16,128]{0,2,1:T(8,128)(2,1)S(1)}, u32[]{:S(2)}, u32[]{:S(2)}) async-start(bf16[256,16,128]{0,2,1:T(8,128)(2,1)} %bitcast.36), calls=%async_computation.1 | async-start | bytes 2097152 | tf_op jit(solution)/shard_map/all_to_all | solution.py:61
  53.8 20.2 %all-to-all-start.2 = ((bf16[256,16,128]{0,2,1:T(8,128)(2,1)}), bf16[256,16,128]{0,2,1:T(8,128)(2,1)S(1)}, u32[]{:S(2)}, u32[]{:S(2)}) async-start(bf16[256,16,128]{0,2,1:T(8,128)(2,1)} %bitcast.228), calls=%async_computation.2 | async-start | bytes 2097152 | tf_op jit(solution)/shard_map/all_to_all | solution.py:62
  74.0 101.9 %all-to-all-start.3 = ((bf16[16,2,512,1,128]{4,2,1,3,0:T(8,128)(2,1)}), bf16[16,2,512,1,128]{4,2,1,3,0:T(8,128)(2,1)}, u32[]{:S(2)}, u32[]{:S(2)}) async-start(bf16[16,2,512,1,128]{4,2,1,3,0:T(8,128)(2,1)} %bitcast.203), calls=%async_computation.3 | async-start | bytes 8388608 | tf_op jit(solution)/shard_map/all_to_all | solution.py:90
  337.0 14.5 %all-to-all-start.4 = ((f32[16,2,1,512]{3,1,2,0:T(2,128)}), f32[16,2,1,512]{3,1,2,0:T(2,128)S(1)}, u32[]{:S(2)}, u32[]{:S(2)}) async-start(f32[16,2,1,512]{3,1,2,0:T(2,128)} %reshape.315), calls=%async_computation.4 | async-start | bytes 131072 | tf_op jit(solution)/shard_map/all_to_all | solution.py:103
  364.0 201.6 %all-to-all-start.5 = ((f32[16,2,512,1,128]{2,4,1,3,0:T(8,128)}), f32[16,2,512,1,128]{2,4,1,3,0:T(8,128)}, u32[]{:S(2)}, u32[]{:S(2)}) async-start(f32[16,2,512,1,128]{2,4,1,3,0:T(8,128)} %bitcast.205), calls=%async_computation.5 | async-start | bytes 16777216 | tf_op jit(solution)/shard_map/all_to_all | solution.py:102
  571.8 3.2 copy-start.1
